TPU v7x, 768 devices: a whole 4x8x12 slice. The times are simulated.
768 devices in a mesh: sec: 12 (over z), tile: 64 (over y, x, core).
Axes of the slice: x: 4, y: 8, z: 12, core: 2. Of those that a mesh axis runs over, the one named last changes fastest.
Arguments:
- atm_tracers: bfloat16 [2, 128, 96, 8192], P(None, None, 'sec', 'tile'), may hold values from -6 to 6
- atm_courant: bfloat16 [128, 96, 8192], P(None, 'sec', 'tile'), may hold values from -0.69921875 to 0.69921875
- atm_diffusion: float32 [128], replicated, may hold values from 0.02 to 0.15
- ocean_tracers: bfloat16 [2, 80, 96, 8192], P(None, None, 'sec', 'tile'), may hold values from -6 to 6
- ocean_courant: bfloat16 [80, 96, 8192], P(None, 'sec', 'tile'), may hold values from -0.5 to 0.5
- ocean_diffusion: float32 [80], replicated, may hold values from 0.02 to 0.15
- surface_seen: float32 [2, 96, 8192], P(None, 'sec', 'tile'), may hold values from -6 to 6
- bulk_coeff: float32 [96, 8192], P('sec', 'tile'), may hold values from 0.2 to 1
- flux_owner: int32 [12, 64, 8, 1], P('sec', 'tile'), may hold values from 0 to 11; in each aligned block of 8 rows (0 to 7, 8 to 15, ..., all dimensions but the last counted through in order) at most 2 rows name the same one
- flux_slot: int32 [12, 64, 8], P('sec', 'tile'), may hold values from 0 to 7
- flux_weight: float32 [12, 64, 8], P('sec', 'tile'), may hold values from 0.5 to 1.5
- ocean_mask: int32 [96, 8192], P('sec', 'tile'), may hold values 0 or 1
Outputs:
- atm_next: bfloat16 [2, 128, 96, 8192], P(None, None, 'sec', 'tile')
- ocean_next: bfloat16 [2, 80, 96, 8192], P(None, None, 'sec', 'tile')
- surface_next: float32 [2, 96, 8192], P(None, 'sec', 'tile')
Inputs may be any that keep to these rules, and one draw needn't show every extreme that they name: `flux_owner`: among the 8 blocks of one device, each owner is named at most 2 times.
All inputs are finite; a program needn't handle non-finite values. No bound on the sum of `ocean_mask` on one device may be relied on, other than what follows from the above.
Results may differ from a plain program's by a relative error of at most 0.0045.
Values may be sent and summed in bfloat16 or wider, within the bound.
A program may use at most 32 MiB of HBM per device.

v0:
```python
import jax
import jax.numpy as jnp
from jax import lax
from jax.sharding import PartitionSpec as P

ATM_STEPS = 3
OCN_STEPS = 2


HIGHEST = lax.Precision.HIGHEST


def extended_2(cells, sides, width):
    for axis, dim in sides:
        count = lax.axis_size(axis)
        head = lax.slice_in_dim(cells, 0, width, axis=dim)
        tail = lax.slice_in_dim(cells, cells.shape[dim] - width, cells.shape[dim], axis=dim)
        cells = jnp.concatenate(
            [
                lax.ppermute(tail, axis, [(i, (i + 1) % count) for i in range(count)]),
                cells,
                lax.ppermute(head, axis, [((i + 1) % count, i) for i in range(count)]),
            ],
            axis=dim,
        )
    return cells


def advance(extended, speed, diffusion):
    center = extended[..., 1:-1]
    right = extended[..., 2:]
    left = extended[..., :-2]
    transport = -0.5 * speed * (right - left) + 0.5 * speed * speed * (right - 2.0 * center + left)
    upper = jnp.concatenate([center[..., :1, :, :], center[..., :-1, :, :]], axis=-3)
    lower = jnp.concatenate([center[..., 1:, :, :], center[..., -1:, :, :]], axis=-3)
    mixing = diffusion[:, None, None] * (upper - 2.0 * center + lower)
    return center + transport + mixing


def body(
    atm_tracers,
    atm_courant,
    atm_diffusion,
    ocean_tracers,
    ocean_courant,
    ocean_diffusion,
    surface_seen,
    bulk_coeff,
    flux_owner,
    flux_slot,
    flux_weight,
    ocean_mask,
):
    atm = atm_tracers.astype(jnp.float32)
    rows = atm.shape[2]
    strip = atm.shape[3]
    rows_ocean = ocean_tracers.shape[2]
    heat = bulk_coeff * (atm[0, -1] - surface_seen[0])
    evap = bulk_coeff * (0.5 * surface_seen[0] - atm[1, -1])
    atm = atm.at[0, -1].add(-0.5 * heat).at[1, -1].add(0.5 * evap)
    payload = jnp.stack([heat, evap]) * flux_weight[0, 0][None, :, None]
    payload = jnp.transpose(payload, (1, 0, 2)).reshape(rows, 2 * strip)
    owner = flux_owner[0, 0, :, 0]
    sections = lax.axis_size("sec")
    capacity = max(2, 2 * rows // sections)
    owner_hot = (owner[:, None] == jnp.arange(sections, dtype=jnp.int32)[None, :]).astype(jnp.int32)
    earlier = jnp.cumsum(owner_hot, axis=0) - owner_hot
    position = owner * capacity + jnp.sum(earlier * owner_hot, axis=1)
    placing = position[:, None] == jnp.arange(sections * capacity, dtype=jnp.int32)[None, :]
    place_float = placing.astype(jnp.float32)
    outgoing = jnp.dot(
        place_float.T, payload, precision=HIGHEST, preferred_element_type=jnp.float32
    )
    outgoing = outgoing.reshape(sections, capacity, 2 * strip)
    slot_ids = jnp.sum(placing.astype(jnp.int32) * (flux_slot[0, 0] + 1)[:, None], axis=0) - 1
    slot_ids = slot_ids.reshape(sections, capacity)
    incoming, incoming_ids = (
        lax.all_to_all(outgoing, "sec", split_axis=0, concat_axis=0, tiled=True),
        lax.all_to_all(slot_ids, "sec", split_axis=0, concat_axis=0, tiled=True),
    )
    collect = (
        incoming_ids.reshape(-1)[None, :] == jnp.arange(rows_ocean, dtype=jnp.int32)[:, None]
    ).astype(jnp.float32)
    flux_rows = jnp.dot(
        collect,
        incoming.reshape(-1, 2 * strip),
        precision=HIGHEST,
        preferred_element_type=jnp.float32,
    )
    flux_ocean = (
        jnp.transpose(flux_rows.reshape(rows_ocean, 2, strip), (1, 0, 2))
        * ocean_mask.astype(jnp.float32)[None]
    )
    ocean = ocean_tracers.astype(jnp.float32)
    ocean = ocean.at[0, 0].add(0.5 * flux_ocean[0]).at[1, 0].add(0.5 * flux_ocean[1])
    atm_speed = atm_courant.astype(jnp.float32)
    ocean_speed = ocean_courant.astype(jnp.float32)
    for repeat in range(ATM_STEPS):
        extended = extended_2(atm, (("tile", 3),), 1)
        atm = advance(extended, atm_speed, atm_diffusion)
    for repeat in range(OCN_STEPS):
        extended = extended_2(ocean, (("tile", 3),), 1)
        ocean = advance(extended, ocean_speed, ocean_diffusion)
    top_rows = jnp.transpose(ocean[:, 0], (1, 0, 2)).reshape(rows_ocean, 2 * strip)
    replies = jnp.dot(collect.T, top_rows, precision=HIGHEST, preferred_element_type=jnp.float32)
    replies = replies.reshape(sections, capacity, 2 * strip)
    answers = lax.all_to_all(replies, "sec", split_axis=0, concat_axis=0, tiled=True)
    surface = jnp.dot(
        place_float,
        answers.reshape(-1, 2 * strip),
        precision=HIGHEST,
        preferred_element_type=jnp.float32,
    )
    surface_next = jnp.transpose(surface.reshape(rows, 2, strip), (1, 0, 2))
    return (atm.astype(jnp.bfloat16), ocean.astype(jnp.bfloat16), surface_next)


def solution(mesh):
    placed = (
        P(None, None, "sec", "tile"),
        P(None, "sec", "tile"),
        P(),
        P(None, None, "sec", "tile"),
        P(None, "sec", "tile"),
        P(),
        P(None, "sec", "tile"),
        P("sec", "tile"),
        P("sec", "tile", None, None),
        P("sec", "tile", None),
        P("sec", "tile", None),
        P("sec", "tile"),
    )
    return jax.shard_map(
        body,
        mesh=mesh,
        in_specs=placed,
        out_specs=(
            P(None, None, "sec", "tile"),
            P(None, None, "sec", "tile"),
            P(None, "sec", "tile"),
        ),
        check_vma=False,
    )
```

profile of v0, /device:TPU:64, one launch (start us, length us, event | category | flops | bytes accessed | tf_op | source)
XLA Modules:
  0.0 156.8 jit_solution(10093547055123888799)
XLA Ops:
  3.8 1.9 %fusion.30 = f32[2,128,8,128]{3,2,1,0:T(8,128)S(1)} fusion(f32[2,128,8,128]{3,2,1,0:T(8,128)S(1)} %copy.107, s32[]{:T(128)} %bitcast, s32[]{:T(128)} %bitcast.1, f32[8,128]{1,0:T(8,128)S(1)} %get-tuple-element.57, pred[]{:T(512)} %and_reduce_fusion), kind=kLoop, calls=%fused_computation.53 | loop fusion | flops 3072 | bytes 12297 | tf_op jit(solution)/shard_map/scatter-add | solution.py:60
  8.7 7.0 %collective-permute-start = (f32[2,128,8,1]{1,2,3,0:T(8,128)S(1)}, f32[2,128,8,1]{1,2,3,0:T(8,128)S(1)}, u32[]{:S(2)}, u32[]{:S(2)}) collective-permute-start(f32[2,128,8,1]{1,2,3,0:T(8,128)S(1)} %copy.71), channel_id=1, source_target_pairs={{1,0},{2,1},{3,2},{4,3},{5,4},{6,5},{7,6},{8,7},{9,8},{10,9},{11,1... | collective-permute-start | bytes 24584 | tf_op jit(solution)/shard_map/ppermute | solution.py:22
  16.1 1.9 %collective-permute-start.1 = (f32[2,128,8,1]{1,2,3,0:T(8,128)S(1)}, f32[2,128,8,1]{1,2,3,0:T(8,128)S(1)}, u32[]{:S(2)}, u32[]{:S(2)}) collective-permute-start(f32[2,128,8,1]{1,2,3,0:T(8,128)S(1)} %copy.73), channel_id=1, source_target_pairs={{0,1},{1,2},{2,3},{3,4},{4,5},{5,6},{6,7},{7,8},{8,9},{9,10},{10,1... | collective-permute-start | bytes 24584 | tf_op jit(solution)/shard_map/ppermute | solution.py:20
  19.8 14.8 %all-to-all-start = ((s32[12,1,2]{2,1,0:T(1,128)}), s32[12,1,2]{2,1,0:T(1,128)S(1)}, u32[]{:S(2)}, u32[]{:S(2)}) async-start(s32[12,1,2]{2,1,0:T(1,128)} %sub.79), calls=%async_computation | async-start | bytes 12288 | tf_op jit(solution)/shard_map/all_to_all | solution.py:79
  40.1 3.0 %all-to-all-done = s32[12,1,2]{2,1,0:T(1,128)S(1)} async-done(((s32[12,1,2]{2,1,0:T(1,128)}), s32[12,1,2]{2,1,0:T(1,128)S(1)}, u32[]{:S(2)}, u32[]{:S(2)}) %all-to-all-start) | async-done | bytes 128 | tf_op jit(solution)/shard_map/all_to_all | solution.py:79
  43.1 6.6 %all-to-all-start.1 = ((f32[12,2,256]{2,1,0:T(2,128)}), f32[12,2,256]{2,1,0:T(2,128)S(1)}, u32[]{:S(2)}, u32[]{:S(2)}) async-start(f32[12,2,256]{2,1,0:T(2,128)} %copy.84), calls=%async_computation.1 | async-start | bytes 49152 | tf_op jit(solution)/shard_map/all_to_all | solution.py:78
  53.9 3.3 %fusion.3 = f32[2,128,8,128]{3,2,1,0:T(8,128)S(1)} fusion(f32[2,127,8,128]{3,2,1,0:T(8,128)} %get-tuple-element.73, f32[2,1,8,128]{3,2,1,0:T(8,128)S(1)} %get-tuple-element.75, f32[2,1,8,128]{3,2,1,0:T(8,128)S(1)} %get-tuple-element.74, f32[2,127,8,128]{3,2,1,0:T(8,128)} %get-tuple-element.72, f32[2,128,8,128]{3,2,1,0:T(8,128)S(1)} %fusion.39, ...), kind=kLoop, calls=%fused_computation.12 | loop fusion | flops 4194304 | bytes 5259776 | tf_op jit(solution)/shard_map/add | solution.py:37
  61.5 5.8 %collective-permute-start.2 = (f32[2,128,8,1]{1,2,3,0:T(8,128)S(1)}, f32[2,128,8,1]{1,2,3,0:T(8,128)S(1)}, u32[]{:S(2)}, u32[]{:S(2)}) collective-permute-start(f32[2,128,8,1]{1,2,3,0:T(8,128)S(1)} %copy.75), channel_id=1, source_target_pairs={{1,0},{2,1},{3,2},{4,3},{5,4},{6,5},{7,6},{8,7},{9,8},{10,9},{11,1... | collective-permute-start | bytes 24584 | tf_op jit(solution)/shard_map/ppermute | solution.py:22
  67.7 1.9 %collective-permute-start.3 = (f32[2,128,8,1]{1,2,3,0:T(8,128)S(1)}, f32[2,128,8,1]{1,2,3,0:T(8,128)S(1)}, u32[]{:S(2)}, u32[]{:S(2)}) collective-permute-start(f32[2,128,8,1]{1,2,3,0:T(8,128)S(1)} %copy.77), channel_id=1, source_target_pairs={{0,1},{1,2},{2,3},{3,4},{4,5},{5,6},{6,7},{7,8},{8,9},{9,10},{10,1... | collective-permute-start | bytes 24584 | tf_op jit(solution)/shard_map/ppermute | solution.py:20
  71.1 5.0 %collective-permute-done.3 = f32[2,128,8,1]{1,2,3,0:T(8,128)S(1)} collective-permute-done((f32[2,128,8,1]{1,2,3,0:T(8,128)S(1)}, f32[2,128,8,1]{1,2,3,0:T(8,128)S(1)}, u32[]{:S(2)}, u32[]{:S(2)}) %collective-permute-start.3) | collective-permute-done | bytes 8224 | tf_op jit(solution)/shard_map/ppermute | solution.py:20
  77.4 3.3 %fusion.6 = f32[2,128,8,128]{3,2,1,0:T(8,128)S(1)} fusion(f32[2,127,8,128]{3,2,1,0:T(8,128)} %get-tuple-element.67, f32[2,1,8,128]{3,2,1,0:T(8,128)S(1)} %get-tuple-element.69, f32[2,1,8,128]{3,2,1,0:T(8,128)S(1)} %get-tuple-element.68, f32[2,127,8,128]{3,2,1,0:T(8,128)} %get-tuple-element.66, f32[2,128,8,128]{3,2,1,0:T(8,128)S(1)} %fusion.3, ...), kind=kLoop, calls=%fused_computation.16 | loop fusion | flops 4194304 | bytes 5259776 | tf_op jit(solution)/shard_map/add | solution.py:37
  85.0 2.0 %collective-permute-start.4 = (f32[2,128,8,1]{1,2,3,0:T(8,128)S(1)}, f32[2,128,8,1]{1,2,3,0:T(8,128)S(1)}, u32[]{:S(2)}, u32[]{:S(2)}) collective-permute-start(f32[2,128,8,1]{1,2,3,0:T(8,128)S(1)} %copy.79), channel_id=1, source_target_pairs={{1,0},{2,1},{3,2},{4,3},{5,4},{6,5},{7,6},{8,7},{9,8},{10,9},{11,1... | collective-permute-start | bytes 24584 | tf_op jit(solution)/shard_map/ppermute | solution.py:22
  87.4 2.3 %collective-permute-start.5 = (f32[2,128,8,1]{1,2,3,0:T(8,128)S(1)}, f32[2,128,8,1]{1,2,3,0:T(8,128)S(1)}, u32[]{:S(2)}, u32[]{:S(2)}) collective-permute-start(f32[2,128,8,1]{1,2,3,0:T(8,128)S(1)} %copy.81), channel_id=1, source_target_pairs={{0,1},{1,2},{2,3},{3,4},{4,5},{5,6},{6,7},{7,8},{8,9},{9,10},{10,1... | collective-permute-start | bytes 24584 | tf_op jit(solution)/shard_map/ppermute | solution.py:20
  91.1 4.6 %collective-permute-done.5 = f32[2,128,8,1]{1,2,3,0:T(8,128)S(1)} collective-permute-done((f32[2,128,8,1]{1,2,3,0:T(8,128)S(1)}, f32[2,128,8,1]{1,2,3,0:T(8,128)S(1)}, u32[]{:S(2)}, u32[]{:S(2)}) %collective-permute-start.5) | collective-permute-done | bytes 8224 | tf_op jit(solution)/shard_map/ppermute | solution.py:20
  99.5 2.0 %collective-permute-start.6 = (f32[2,80,8,1]{1,2,3,0:T(8,128)}, f32[2,80,8,1]{1,2,3,0:T(8,128)S(1)}, u32[]{:S(2)}, u32[]{:S(2)}) collective-permute-start(f32[2,80,8,1]{1,2,3,0:T(8,128)} %copy.86), channel_id=1, source_target_pairs={{1,0},{2,1},{3,2},{4,3},{5,4},{6,5},{7,6},{8,7},{9,8},{10,9},{11,1... | collective-permute-start | bytes 15368 | tf_op jit(solution)/shard_map/ppermute | solution.py:22
  102.3 2.3 %collective-permute-start.7 = (f32[2,80,8,1]{1,2,3,0:T(8,128)}, f32[2,80,8,1]{1,2,3,0:T(8,128)S(1)}, u32[]{:S(2)}, u32[]{:S(2)}) collective-permute-start(f32[2,80,8,1]{1,2,3,0:T(8,128)} %copy.88), channel_id=1, source_target_pairs={{0,1},{1,2},{2,3},{3,4},{4,5},{5,6},{6,7},{7,8},{8,9},{9,10},{10,1... | collective-permute-start | bytes 15368 | tf_op jit(solution)/shard_map/ppermute | solution.py:20
  106.4 4.4 %collective-permute-done.7 = f32[2,80,8,1]{1,2,3,0:T(8,128)S(1)} collective-permute-done((f32[2,80,8,1]{1,2,3,0:T(8,128)}, f32[2,80,8,1]{1,2,3,0:T(8,128)S(1)}, u32[]{:S(2)}, u32[]{:S(2)}) %collective-permute-start.7) | collective-permute-done | bytes 5152 | tf_op jit(solution)/shard_map/ppermute | solution.py:20
  112.7 2.3 %fusion.13 = f32[2,80,8,128]{3,2,1,0:T(8,128)S(1)} fusion(f32[2,79,8,128]{3,2,1,0:T(8,128)} %get-tuple-element.85, f32[2,1,8,128]{3,2,1,0:T(8,128)} %get-tuple-element.87, f32[2,1,8,128]{3,2,1,0:T(8,128)S(1)} %copy-done.6, f32[2,79,8,128]{3,2,1,0:T(8,128)} %get-tuple-element.84, f32[2,80,8,128]{3,2,1,0:T(8,128)S(1)} %fusion.33, f32[2,80,8,1]{3,2,1,0:T(8,128)} %copy.87, ...), kind=kLoop, calls=%fused_computation.31 | loop fusion | flops 2621440 | bytes 3287360 | tf_op jit(solution)/shard_map/add | solution.py:37
  117.2 1.9 %copy.92 = f32[2,80,8,1]{1,2,3,0:T(8,128)} copy(f32[2,80,8,1]{3,2,1,0:T(8,128)} %get-tuple-element.77) | data formatting | bytes 10240 | tf_op jit(solution)/shard_map/slice | solution.py:17
  121.9 7.1 %collective-permute-start.8 = (f32[2,80,8,1]{1,2,3,0:T(8,128)}, f32[2,80,8,1]{1,2,3,0:T(8,128)S(1)}, u32[]{:S(2)}, u32[]{:S(2)}) collective-permute-start(f32[2,80,8,1]{1,2,3,0:T(8,128)} %copy.90), channel_id=1, source_target_pairs={{1,0},{2,1},{3,2},{4,3},{5,4},{6,5},{7,6},{8,7},{9,8},{10,9},{11,1... | collective-permute-start | bytes 15368 | tf_op jit(solution)/shard_map/ppermute | solution.py:22
  132.7 3.1 %fusion.55 = (bf16[2,80,8,128]{3,2,1,0:T(8,128)(2,1)}, f32[2,80,8,128]{3,2,1,0:T(8,128)S(1)}) fusion(f32[2,1,8,128]{3,2,1,0:T(8,128)S(1)} %get-tuple-element.79, f32[2,79,8,128]{3,2,1,0:T(8,128)} %get-tuple-element.81, f32[2,79,8,128]{3,2,1,0:T(8,128)} %get-tuple-element.80, f32[2,1,8,128]{3,2,1,0:T(8,128)S(1)} %get-tuple-element.78, f32[80]{0:T(128)S(1)} %copy-done.14, ...), kind=kLoop, calls=%fused_computation.93 | loop fusion | flops 2785280 | bytes 3615040 | tf_op jit(solution)/shard_map/convert_element_type | solution.py:115
  137.4 9.6 %all-to-all-start.2 = ((f32[12,2,256]{2,1,0:T(2,128)}), f32[12,2,256]{2,1,0:T(2,128)S(1)}, u32[]{:S(2)}, u32[]{:S(2)}) async-start(f32[12,2,256]{2,1,0:T(2,128)} %copy.95), calls=%async_computation.2 | async-start | bytes 49152 | tf_op jit(solution)/shard_map/all_to_all | solution.py:107
  147.6 4.0 %fusion.10 = bf16[2,128,8,128]{3,2,1,0:T(8,128)(2,1)} fusion(f32[2,127,8,128]{3,2,1,0:T(8,128)} %get-tuple-element.61, f32[2,1,8,128]{3,2,1,0:T(8,128)S(1)} %get-tuple-element.63, f32[2,1,8,128]{3,2,1,0:T(8,128)S(1)} %get-tuple-element.62, f32[2,127,8,128]{3,2,1,0:T(8,128)} %get-tuple-element.60, f32[2,128,8,128]{3,2,1,0:T(8,128)S(1)} %fusion.6, ...), kind=kLoop, calls=%fused_computation.21 | loop fusion | flops 4456448 | bytes 4735488 | tf_op jit(solution)/shard_map/convert_element_type | solution.py:115
  151.6 4.4 %all-to-all-done.2 = f32[12,2,256]{2,1,0:T(2,128)S(1)} async-done(((f32[12,2,256]{2,1,0:T(2,128)}), f32[12,2,256]{2,1,0:T(2,128)S(1)}, u32[]{:S(2)}, u32[]{:S(2)}) %all-to-all-start.2) | async-done | bytes 24608 | tf_op jit(solution)/shard_map/all_to_all | solution.py:107
  (118 shorter events, 51.0 us)
Async XLA Ops:
  1.8 0.7 copy-start.8
  8.7 41.8 %collective-permute-start = (f32[2,128,8,1]{1,2,3,0:T(8,128)S(1)}, f32[2,128,8,1]{1,2,3,0:T(8,128)S(1)}, u32[]{:S(2)}, u32[]{:S(2)}) collective-permute-start(f32[2,128,8,1]{1,2,3,0:T(8,128)S(1)} %copy.71), channel_id=1, source_target_pairs={{1,0},{2,1},{3,2},{4,3},{5,4},{6,5},{7,6},{8,7},{9,8},{10,9},{11,1... | collective-permute-start | bytes 24584 | tf_op jit(solution)/shard_map/ppermute | solution.py:22
  15.7 2.3 %copy-start.17 = (s32[1,1,8]{2,1,0:T(1,128)S(1)}, s32[1,1,8]{2,1,0:T(1,128)}, u32[]{:S(2)}) copy-start(s32[1,1,8]{2,1,0:T(1,128)} %param.29) | copy-start | bytes 100
  16.1 35.8 %collective-permute-start.1 = (f32[2,128,8,1]{1,2,3,0:T(8,128)S(1)}, f32[2,128,8,1]{1,2,3,0:T(8,128)S(1)}, u32[]{:S(2)}, u32[]{:S(2)}) collective-permute-start(f32[2,128,8,1]{1,2,3,0:T(8,128)S(1)} %copy.73), channel_id=1, source_target_pairs={{0,1},{1,2},{2,3},{3,4},{4,5},{5,6},{6,7},{7,8},{8,9},{9,10},{10,1... | collective-permute-start | bytes 24584 | tf_op jit(solution)/shard_map/ppermute | solution.py:20
  19.0 18.8 %copy-start.19 = (s32[8]{0:T(128)}, s32[8]{0:T(128)S(1)}, u32[]{:S(2)}) copy-start(s32[8]{0:T(128)S(1)} %multiply_add_fusion.1) | copy-start | bytes 100
  19.8 23.3 %all-to-all-start = ((s32[12,1,2]{2,1,0:T(1,128)}), s32[12,1,2]{2,1,0:T(1,128)S(1)}, u32[]{:S(2)}, u32[]{:S(2)}) async-start(s32[12,1,2]{2,1,0:T(1,128)} %sub.79), calls=%async_computation | async-start | bytes 12288 | tf_op jit(solution)/shard_map/all_to_all | solution.py:79
  34.5 1.5 copy-start.4
  36.0 0.9 copy-start.5
  36.9 1.8 %copy-start.3 = (bf16[2,80,8,128]{3,2,1,0:T(8,128)(2,1)S(1)}, bf16[2,80,8,128]{3,2,1,0:T(8,128)(2,1)}, u32[]{:S(2)}) copy-start(bf16[2,80,8,128]{3,2,1,0:T(8,128)(2,1)} %param.23) | copy-start | bytes 983044
  43.1 53.9 %all-to-all-start.1 = ((f32[12,2,256]{2,1,0:T(2,128)}), f32[12,2,256]{2,1,0:T(2,128)S(1)}, u32[]{:S(2)}, u32[]{:S(2)}) async-start(f32[12,2,256]{2,1,0:T(2,128)} %copy.84), calls=%async_computation.1 | async-start | bytes 49152 | tf_op jit(solution)/shard_map/all_to_all | solution.py:78
  61.5 8.2 %collective-permute-start.2 = (f32[2,128,8,1]{1,2,3,0:T(8,128)S(1)}, f32[2,128,8,1]{1,2,3,0:T(8,128)S(1)}, u32[]{:S(2)}, u32[]{:S(2)}) collective-permute-start(f32[2,128,8,1]{1,2,3,0:T(8,128)S(1)} %copy.75), channel_id=1, source_target_pairs={{1,0},{2,1},{3,2},{4,3},{5,4},{6,5},{7,6},{8,7},{9,8},{10,9},{11,1... | collective-permute-start | bytes 24584 | tf_op jit(solution)/shard_map/ppermute | solution.py:22
  67.7 8.3 %collective-permute-start.3 = (f32[2,128,8,1]{1,2,3,0:T(8,128)S(1)}, f32[2,128,8,1]{1,2,3,0:T(8,128)S(1)}, u32[]{:S(2)}, u32[]{:S(2)}) collective-permute-start(f32[2,128,8,1]{1,2,3,0:T(8,128)S(1)} %copy.77), channel_id=1, source_target_pairs={{0,1},{1,2},{2,3},{3,4},{4,5},{5,6},{6,7},{7,8},{8,9},{9,10},{10,1... | collective-permute-start | bytes 24584 | tf_op jit(solution)/shard_map/ppermute | solution.py:20
  85.0 4.7 %collective-permute-start.4 = (f32[2,128,8,1]{1,2,3,0:T(8,128)S(1)}, f32[2,128,8,1]{1,2,3,0:T(8,128)S(1)}, u32[]{:S(2)}, u32[]{:S(2)}) collective-permute-start(f32[2,128,8,1]{1,2,3,0:T(8,128)S(1)} %copy.79), channel_id=1, source_target_pairs={{1,0},{2,1},{3,2},{4,3},{5,4},{6,5},{7,6},{8,7},{9,8},{10,9},{11,1... | collective-permute-start | bytes 24584 | tf_op jit(solution)/shard_map/ppermute | solution.py:22
  87.4 8.3 %collective-permute-start.5 = (f32[2,128,8,1]{1,2,3,0:T(8,128)S(1)}, f32[2,128,8,1]{1,2,3,0:T(8,128)S(1)}, u32[]{:S(2)}, u32[]{:S(2)}) collective-permute-start(f32[2,128,8,1]{1,2,3,0:T(8,128)S(1)} %copy.81), channel_id=1, source_target_pairs={{0,1},{1,2},{2,3},{3,4},{4,5},{5,6},{6,7},{7,8},{8,9},{9,10},{10,1... | collective-permute-start | bytes 24584 | tf_op jit(solution)/shard_map/ppermute | solution.py:20
  99.5 5.8 %collective-permute-start.6 = (f32[2,80,8,1]{1,2,3,0:T(8,128)}, f32[2,80,8,1]{1,2,3,0:T(8,128)S(1)}, u32[]{:S(2)}, u32[]{:S(2)}) collective-permute-start(f32[2,80,8,1]{1,2,3,0:T(8,128)} %copy.86), channel_id=1, source_target_pairs={{1,0},{2,1},{3,2},{4,3},{5,4},{6,5},{7,6},{8,7},{9,8},{10,9},{11,1... | collective-permute-start | bytes 15368 | tf_op jit(solution)/shard_map/ppermute | solution.py:22
  102.3 8.5 %collective-permute-start.7 = (f32[2,80,8,1]{1,2,3,0:T(8,128)}, f32[2,80,8,1]{1,2,3,0:T(8,128)S(1)}, u32[]{:S(2)}, u32[]{:S(2)}) collective-permute-start(f32[2,80,8,1]{1,2,3,0:T(8,128)} %copy.88), channel_id=1, source_target_pairs={{0,1},{1,2},{2,3},{3,4},{4,5},{5,6},{6,7},{7,8},{8,9},{9,10},{10,1... | collective-permute-start | bytes 15368 | tf_op jit(solution)/shard_map/ppermute | solution.py:20
  106.4 5.6 %copy-start.1 = (f32[80,8,128]{2,1,0:T(8,128)S(1)}, f32[80,8,128]{2,1,0:T(8,128)}, u32[]{:S(2)}) copy-start(f32[80,8,128]{2,1,0:T(8,128)} %get-tuple-element.90) | copy-start | bytes 983044
  106.4 5.6 %copy-start.2 = (f32[80,8,128]{2,1,0:T(8,128)S(1)}, f32[80,8,128]{2,1,0:T(8,128)}, u32[]{:S(2)}) copy-start(f32[80,8,128]{2,1,0:T(8,128)} %get-tuple-element.91) | copy-start | bytes 983044
  112.0 0.7 copy-start.13
  119.2 9.9 %collective-permute-start.9 = (f32[2,80,8,1]{1,2,3,0:T(8,128)}, f32[2,80,8,1]{1,2,3,0:T(8,128)}, u32[]{:S(2)}, u32[]{:S(2)}) collective-permute-start(f32[2,80,8,1]{1,2,3,0:T(8,128)} %copy.92), channel_id=1, source_target_pairs={{0,1},{1,2},{2,3},{3,4},{4,5},{5,6},{6,7},{7,8},{8,9},{9,10},{10,1... | collective-permute-start | bytes 15368 | tf_op jit(solution)/shard_map/ppermute | solution.py:20
  121.9 9.0 %collective-permute-start.8 = (f32[2,80,8,1]{1,2,3,0:T(8,128)}, f32[2,80,8,1]{1,2,3,0:T(8,128)S(1)}, u32[]{:S(2)}, u32[]{:S(2)}) collective-permute-start(f32[2,80,8,1]{1,2,3,0:T(8,128)} %copy.90), channel_id=1, source_target_pairs={{1,0},{2,1},{3,2},{4,3},{5,4},{6,5},{7,6},{8,7},{9,8},{10,9},{11,1... | collective-permute-start | bytes 15368 | tf_op jit(solution)/shard_map/ppermute | solution.py:22
  132.7 14.2 %copy-start = (f32[128,8,128]{2,1,0:T(8,128)S(1)}, f32[128,8,128]{2,1,0:T(8,128)}, u32[]{:S(2)}) copy-start(f32[128,8,128]{2,1,0:T(8,128)} %get-tuple-element.89) | copy-start | bytes 1572868
  137.4 18.6 %all-to-all-start.2 = ((f32[12,2,256]{2,1,0:T(2,128)}), f32[12,2,256]{2,1,0:T(2,128)S(1)}, u32[]{:S(2)}, u32[]{:S(2)}) async-start(f32[12,2,256]{2,1,0:T(2,128)} %copy.95), calls=%async_computation.2 | async-start | bytes 49152 | tf_op jit(solution)/shard_map/all_to_all | solution.py:107
  151.6 4.4 %copy-start.20 = (s32[8]{0:T(128)S(1)}, s32[8]{0:T(128)}, u32[]{:S(2)}) copy-start(s32[8]{0:T(128)} %copy-done.19) | copy-start | bytes 100
  (10 other events, 6.7 us)
where the time goes:
time: 158 us; the launch traced here: 157 us
  starting transfers between devices  65.4 us (41%)
  local copies, waits for them, and re-layouts  45.6 us (29%)
  other arithmetic  22.1 us (14%)
  waiting for transfers between devices  21.4 us (14%)
    ppermute x5, starting transfers between devices, extended_2(): lax.ppermute(head, axis, [((i + 1) % count, i) for i in range(count)])  24 us
    all_to_all x1, starting transfers between devices, body(): lax.all_to_all(slot_ids, 'sec', split_axis=0, concat_axis=0, tiled=True)  14.8 us
    ppermute x5, waiting for transfers between devices, extended_2(): lax.ppermute(tail, axis, [(i, (i + 1) % count) for i in range(count)])  14 us
    ppermute x5, starting transfers between devices, extended_2(): lax.ppermute(tail, axis, [(i, (i + 1) % count) for i in range(count)])  10.4 us
    all_to_all x1, starting transfers between devices, body(): lax.all_to_all(replies, 'sec', split_axis=0, concat_axis=0, tiled=True)  9.62 us
    add x3, other arithmetic, advance(): return center + transport + mixing  8.97 us
    slice x9, local copies, waits for them, and re-layouts, extended_2(): lax.slice_in_dim(cells, cells.shape[dim] - width, cells.shape[dim], axis=...  8.04 us
    slice x6, local copies, waits for them, and re-layouts, extended_2(): head = lax.slice_in_dim(cells, 0, width, axis=dim)  7.45 us
  transfers between devices with their start and end apart: 13, of which 5 were waited for; matrix products, arithmetic and copies ran while one was open for 25% of the time, Pallas kernels for 0%

commit v1 on v0

v1 whole, which is shorter than its diff:
```python
import jax
import jax.numpy as jnp
from jax import lax
from jax.experimental import pallas as pl
from jax.experimental.pallas import tpu as pltpu
from jax.sharding import PartitionSpec as P

ATM_STEPS = 3
OCN_STEPS = 2
SEC = 12
TILE = 64
ROWS = 8
LANES = 128
LA = 128
LO = 80
GROUP = 16
CHUNK = 8
F32 = jnp.float32
BF16 = jnp.bfloat16
MESH = pl.DeviceIdType.MESH

PA, PAC, PO, POC = 0, 2 * LA // GROUP, 3 * LA // GROUP, (3 * LA + 2 * LO) // GROUP
PACKED = (3 * LA + 3 * LO) // GROUP


def lane_ids():
    return lax.broadcasted_iota(jnp.int32, (ROWS, LANES), 1)


def shifted(main, halo, lane):
    rm, rh = pltpu.roll(main, LANES - 1, 1), pltpu.roll(halo, LANES - 1, 1)
    lm, lh = pltpu.roll(main, 1, 1), pltpu.roll(halo, 1, 1)
    last, first = lane == LANES - 1, lane == 0
    return (
        (jnp.where(last, rh, rm), jnp.where(first, lh, lm)),
        (jnp.where(last, rm, rh), jnp.where(first, lm, lh)),
    )


def cell_step(q, up, dn, right, left, c, k):
    twice = 2.0 * q
    transport = (0.5 * c) * (c * ((right + left) - twice) - (right - left))
    return q + transport + k * ((up + dn) - twice)


def level_step(src_m, src_h, f, l, c_m, c_h, k, lane, with_halo):
    m, h = src_m[f, l + 1], src_h[f, l + 1]
    (rm, lm), (rh, lh) = shifted(m, h, lane)
    new_m = cell_step(m, src_m[f, l], src_m[f, l + 2], rm, lm, c_m, k)
    new_h = None
    if with_halo:
        new_h = cell_step(h, src_h[f, l], src_h[f, l + 2], rh, lh, c_h, k)
    return new_m, new_h


def step_levels(src_m, src_h, dst_m, dst_h, cm_ref, ch_ref, k_ref, levels, out=None):
    @pl.loop(0, levels // CHUNK)
    def _(i):
        lane = lane_ids()
        for g in range(CHUNK):
            l = i * CHUNK + g
            c_m = cm_ref[l].astype(F32)
            c_h = ch_ref[l]
            k = k_ref[l]
            for f in range(2):
                new_m, new_h = level_step(
                    src_m, src_h, f, l, c_m, c_h, k, lane, out is None
                )
                if out is None:
                    dst_m[f, l + 1] = new_m
                    dst_h[f, l + 1] = new_h
                else:
                    out[f, l] = new_m.astype(BF16)

    if out is None:
        pad_levels(dst_m, levels)
        pad_levels(dst_h, levels)


def pad_levels(ref, levels):
    for f in range(2):
        ref[f, 0] = ref[f, 1]
        ref[f, levels + 1] = ref[f, levels]


def widen(src, dst, levels):
    @pl.loop(0, levels // CHUNK)
    def _(i):
        for g in range(CHUNK):
            l = i * CHUNK + g
            for f in range(2):
                dst[f, l + 1] = src[f, l].astype(F32)


def pack_edges(read, groups, base, packed):
    @pl.loop(0, groups)
    def _(i):
        part = lane_ids() // 8
        acc = jnp.zeros((ROWS, LANES), F32)
        for j in range(GROUP):
            rolled = pltpu.roll(read(i * GROUP + j), (8 * j + 4) % LANES, 1)
            acc = jnp.where(part == j, rolled, acc)
        packed[base + i] = acc.astype(BF16)


def unpack_edges(store, groups, base, from_left, from_right):
    @pl.loop(0, groups)
    def _(i):
        lane = lane_ids()
        both = jnp.where(
            lane % 8 < 4,
            from_left[base + i].astype(F32),
            from_right[base + i].astype(F32),
        )
        for j in range(GROUP):
            store(i * GROUP + j, pltpu.roll(both, (LANES - 8 * j - 4) % LANES, 1))


def kernel(
    atm_h, acour_h, adiff_h, ocn_h, ocour_h, odiff_h, seen_h, bulk_h, mask_h, meta,
    atm_o, ocn_o, surf_o,
    atm_in, acour, adiff, ocn_in, ocour, odiff, seen, bulk, mask,
    a0m, a0h, a1m, a1h, o0m, o0h, o1m, o1h, acour_e, ocour_e,
    packed, from_left, from_right,
    flux_out, flux_in, reply_out, reply_in, edge_out, edge_left, edge_right,
    in_sem, flux_ss, flux_rs, reply_ss, reply_rs, halo_ss, halo_rs, edge_ss, edge_rs,
):
    sec = lax.axis_index("sec")
    tile = lax.axis_index("tile")
    to_left = (sec, lax.rem(tile + TILE - 1, TILE))
    to_right = (sec, lax.rem(tile + 1, TILE))
    order = sorted(range(1, SEC), key=lambda k: -min(k, SEC - k))

    barrier = pltpu.get_barrier_semaphore()
    for k in order:
        pl.semaphore_signal(
            barrier, inc=1, device_id=(lax.rem(sec + k, SEC), tile), device_id_type=MESH
        )
    for where in (to_left, to_right):
        pl.semaphore_signal(barrier, inc=1, device_id=where, device_id_type=MESH)

    pairs = [
        (atm_h, atm_in), (seen_h, seen), (bulk_h, bulk), (acour_h, acour),
        (ocn_h, ocn_in), (ocour_h, ocour), (mask_h, mask), (adiff_h, adiff),
        (odiff_h, odiff),
    ]
    loads = [
        pltpu.make_async_copy(src, dst, in_sem.at[i]) for i, (src, dst) in enumerate(pairs)
    ]
    for load in loads:
        load.start()

    lane = lane_ids()
    row = lax.broadcasted_iota(jnp.int32, (ROWS, LANES), 0)

    owner_row, owner_lane = meta[0], meta[1]
    earlier = jnp.sum(
        jnp.where((owner_row == owner_lane) & (row < lane % 8), 1.0, 0.0),
        axis=0,
        keepdims=True,
    )
    target = 8.0 * owner_lane[0:1] + 2.0 * (lane[0:1] // 8).astype(F32) + earlier
    target = jnp.where(lane[0:1] < 24, target, -1.0)
    rows_all = lax.broadcasted_iota(jnp.int32, (8 * SEC, LANES), 0)
    placing = jnp.where(rows_all.astype(F32) == target, 1.0, 0.0)

    for load in loads[:3]:
        load.wait()
    top_t = atm_in[0, LA - 1].astype(F32)
    top_q = atm_in[1, LA - 1].astype(F32)
    heat = bulk[...] * (top_t - seen[0])
    evap = bulk[...] * (0.5 * seen[0] - top_q)
    weight = meta[3]
    payload = jnp.concatenate(
        [heat * weight, evap * weight, meta[2] + 1.0, jnp.zeros((LANES - 24, LANES), F32)],
        axis=0,
    )
    outgoing = jnp.dot(
        placing.astype(BF16), payload.astype(BF16), preferred_element_type=F32
    )
    flux_out[...] = outgoing.reshape(SEC, ROWS, LANES).astype(BF16)
    flux_in[sec] = flux_out[sec]

    widen(atm_in, a0m, LA)
    a0m[0, LA] = top_t - 0.5 * heat
    a0m[1, LA] = top_q + 0.5 * evap
    pad_levels(a0m, LA)
    for load in loads[3:]:
        load.wait()
    widen(ocn_in, o0m, LO)
    pad_levels(o0m, LO)
    for f in range(2):
        pack_edges(lambda l, f=f: a0m[f, l + 1], LA // GROUP, PA + f * LA // GROUP, packed)
        pack_edges(lambda l, f=f: o0m[f, l + 1], LO // GROUP, PO + f * LO // GROUP, packed)
    pack_edges(lambda l: acour[l].astype(F32), LA // GROUP, PAC, packed)
    pack_edges(lambda l: ocour[l].astype(F32), LO // GROUP, POC, packed)

    pl.semaphore_wait(barrier, SEC + 1)

    def to_sec(k, src, dst, ss, rs):
        peer = lax.rem(sec + k, SEC)
        return pltpu.make_async_remote_copy(
            src_ref=src.at[peer], dst_ref=dst.at[sec], send_sem=ss.at[k], recv_sem=rs.at[k],
            device_id=(peer, tile), device_id_type=MESH,
        )

    def to_sides(src, at_left, at_right, ss, rs):
        return [
            pltpu.make_async_remote_copy(
                src_ref=src, dst_ref=dst, send_sem=ss.at[i], recv_sem=rs.at[i],
                device_id=where, device_id_type=MESH,
            )
            for i, (dst, where) in enumerate(((at_left, to_right), (at_right, to_left)))
        ]

    fluxes = [to_sec(k, flux_out, flux_in, flux_ss, flux_rs) for k in order]
    for copy in fluxes:
        copy.start()
    halos = to_sides(packed, from_left, from_right, halo_ss, halo_rs)
    for copy in halos:
        copy.start()
    for copy in halos:
        copy.wait()

    def put_a(f):
        def store(l, value):
            a0h[f, l + 1] = value
        return store

    def put_o(f):
        def store(l, value):
            o0h[f, l + 1] = value
        return store

    def put_ac(l, value):
        acour_e[l] = value

    def put_oc(l, value):
        ocour_e[l] = value

    for f in range(2):
        unpack_edges(put_o(f), LO // GROUP, PO + f * LO // GROUP, from_left, from_right)
    unpack_edges(put_oc, LO // GROUP, POC, from_left, from_right)
    pad_levels(o0h, LO)
    step_levels(o0m, o0h, o1m, o1h, ocour, ocour_e, odiff, LO)
    for f in range(2):
        unpack_edges(put_a(f), LA // GROUP, PA + f * LA // GROUP, from_left, from_right)
    unpack_edges(put_ac, LA // GROUP, PAC, from_left, from_right)
    pad_levels(a0h, LA)
    step_levels(a0m, a0h, a1m, a1h, acour, acour_e, adiff, LA)

    for copy in fluxes:
        copy.wait()
    arrived = flux_in[...].astype(F32).reshape(8 * SEC, LANES)
    lane_all = lax.broadcasted_iota(jnp.int32, (8 * SEC, LANES), 1)
    kind = rows_all % 8
    up2 = pltpu.roll(arrived, 8 * SEC - 2, 0)
    up4 = pltpu.roll(arrived, 8 * SEC - 4, 0)
    slot = (lane_all % 8 + 1).astype(F32)
    collect = jnp.where(
        ((kind < 2) & (lane_all < 8) & (up4 == slot))
        | ((kind >= 2) & (kind < 4) & (lane_all >= 8) & (lane_all < 16) & (up2 == slot)),
        1.0,
        0.0,
    )
    received = lax.dot_general(
        collect.astype(BF16), arrived.astype(BF16), (((0,), (0,)), ((), ())),
        preferred_element_type=F32,
    )
    half = 0.5 * mask[...].astype(F32)
    added = [half * received[8 * f : 8 * f + 8] for f in range(2)]
    for f in range(2):
        edge_out[f] = added[f].astype(BF16)
        o0m[f, 1] = o0m[f, 1] + added[f]
        o0m[f, 0] = o0m[f, 1]
    edges = to_sides(edge_out, edge_left, edge_right, edge_ss, edge_rs)
    for copy in edges:
        copy.start()
    for copy in edges:
        copy.wait()
    for f in range(2):
        outer = jnp.where(
            lane < 4,
            edge_right[f].astype(F32),
            jnp.where(lane >= LANES - 4, edge_left[f].astype(F32), 0.0),
        )
        o0h[f, 1] = o0h[f, 1] + outer
        o0h[f, 0] = o0h[f, 1]
    for l in range(2):
        for f in range(2):
            new_m, new_h = level_step(
                o0m, o0h, f, l, ocour[l].astype(F32), ocour_e[l], odiff[l], lane, True
            )
            o1m[f, l + 1] = new_m
            o1h[f, l + 1] = new_h
    tops = []
    for f in range(2):
        o1m[f, 0] = o1m[f, 1]
        top, _ = level_step(
            o1m, o1h, f, 0, ocour[0].astype(F32), ocour_e[0], odiff[0], lane, False
        )
        tops.append(top)
    rows_top = jnp.concatenate(tops + [jnp.zeros((LANES - 16, LANES), F32)], axis=0)
    answers = jnp.dot(collect.astype(BF16), rows_top.astype(BF16), preferred_element_type=F32)
    reply_out[...] = answers.reshape(SEC, ROWS, LANES).astype(BF16)
    replies = [to_sec(k, reply_out, reply_in, reply_ss, reply_rs) for k in order]
    for copy in replies:
        copy.start()
    reply_in[sec] = reply_out[sec]

    step_levels(o1m, o1h, None, None, ocour, ocour_e, odiff, LO, ocn_o)
    step_levels(a1m, a1h, a0m, a0h, acour, acour_e, adiff, LA)
    step_levels(a0m, a0h, None, None, acour, acour_e, adiff, LA, atm_o)

    for copy in replies:
        copy.wait()
    back = reply_in[...].astype(F32).reshape(8 * SEC, LANES)
    surface = lax.dot_general(
        placing.astype(BF16), back.astype(BF16), (((0,), (0,)), ((), ())),
        preferred_element_type=F32,
    )
    surf_o[0] = surface[0:8]
    surf_o[1] = surface[8:16]


def body(
    atm_tracers, atm_courant, atm_diffusion, ocean_tracers, ocean_courant, ocean_diffusion,
    surface_seen, bulk_coeff, flux_owner, flux_slot, flux_weight, ocean_mask,
):
    shape = (ROWS, LANES)
    owner = flux_owner[0, 0, :, 0].astype(F32)
    by_lane = jnp.pad(jnp.tile(owner, 3), (0, LANES - 24), constant_values=-1.0)
    meta = jnp.stack(
        [
            jnp.broadcast_to(owner[:, None], shape),
            jnp.broadcast_to(by_lane[None, :], shape),
            jnp.broadcast_to(flux_slot[0, 0].astype(F32)[:, None], shape),
            jnp.broadcast_to(flux_weight[0, 0][:, None], shape),
        ]
    )
    hbm = pl.BlockSpec(memory_space=pl.ANY)
    vmem = pl.BlockSpec(memory_space=pltpu.VMEM)
    V = pltpu.VMEM
    D = pltpu.SemaphoreType.DMA
    strip_a, strip_o = V((2, LA + 2) + shape, F32), V((2, LO + 2) + shape, F32)
    return pl.pallas_call(
        kernel,
        out_shape=(
            jax.ShapeDtypeStruct((2, LA) + shape, BF16),
            jax.ShapeDtypeStruct((2, LO) + shape, BF16),
            jax.ShapeDtypeStruct((2,) + shape, F32),
        ),
        in_specs=[hbm] * 9 + [vmem],
        out_specs=(vmem, vmem, vmem),
        scratch_shapes=[
            V((2, LA) + shape, BF16), V((LA,) + shape, BF16), pltpu.SMEM((LA,), F32),
            V((2, LO) + shape, BF16), V((LO,) + shape, BF16), pltpu.SMEM((LO,), F32),
            V((2,) + shape, F32), V(shape, F32), V(shape, jnp.int32),
            strip_a, strip_a, strip_a, strip_a, strip_o, strip_o, strip_o, strip_o,
            V((LA,) + shape, F32), V((LO,) + shape, F32),
            V((PACKED,) + shape, BF16), V((PACKED,) + shape, BF16), V((PACKED,) + shape, BF16),
            V((SEC,) + shape, BF16), V((SEC,) + shape, BF16),
            V((SEC,) + shape, BF16), V((SEC,) + shape, BF16),
            V((2,) + shape, BF16), V((2,) + shape, BF16), V((2,) + shape, BF16),
            D((9,)), D((SEC,)), D((SEC,)), D((SEC,)), D((SEC,)),
            D((2,)), D((2,)), D((2,)), D((2,)),
        ],
        compiler_params=pltpu.CompilerParams(collective_id=0, has_side_effects=True),
        name="coupled_window",
    )(
        atm_tracers, atm_courant, atm_diffusion, ocean_tracers, ocean_courant,
        ocean_diffusion, surface_seen, bulk_coeff, ocean_mask, meta,
    )


def solution(mesh):
    placed = (
        P(None, None, "sec", "tile"),
        P(None, "sec", "tile"),
        P(),
        P(None, None, "sec", "tile"),
        P(None, "sec", "tile"),
        P(),
        P(None, "sec", "tile"),
        P("sec", "tile"),
        P("sec", "tile", None, None),
        P("sec", "tile", None),
        P("sec", "tile", None),
        P("sec", "tile"),
    )
    return jax.shard_map(
        body,
        mesh=mesh,
        in_specs=placed,
        out_specs=(
            P(None, None, "sec", "tile"),
            P(None, None, "sec", "tile"),
            P(None, "sec", "tile"),
        ),
        check_vma=False,
    )
```

time: 158 us -> 46.6 us (0.29)
  the two profiles are of different devices: /device:TPU:64 before, /device:TPU:1 now
where the time goes in v1:
time: 46.6 us; the launch traced here: 46.2 us
  Pallas kernels  39.5 us (85%)
  local copies, waits for them, and re-layouts  5.44 us (12%)
  between operations  0.66 us (1%)
  other arithmetic  0.61 us (1%)
    pallas_call x1, Pallas kernels, body(): pl.pallas_call(kernel, out_shape=(jax.ShapeDtypeStruct((2, LA) + shape, B...  39.5 us
    unnamed x13, local copies, waits for them, and re-layouts  5.13 us

profile of v1, /device:TPU:1, one launch (start us, length us, event | category | flops | bytes accessed | tf_op | source)
XLA Modules:
  0.0 46.2 jit_solution(5267528880861757422)
XLA Ops:
  0.6 0.0 copy-start.3
  0.6 0.6 %copy-done.3 = s32[1,1,8,1]{2,3,1,0:T(1,128)S(1)} copy-done((s32[1,1,8,1]{2,3,1,0:T(1,128)S(1)}, s32[1,1,8,1]{2,3,1,0:T(1,128)}, u32[]{:S(2)}) %copy-start.3) | copy-done | bytes 56
  1.3 0.0 copy-start.4
  1.3 0.7 %copy-done.4 = s32[1,1,8]{2,1,0:T(1,128)S(1)} copy-done((s32[1,1,8]{2,1,0:T(1,128)S(1)}, s32[1,1,8]{2,1,0:T(1,128)}, u32[]{:S(2)}) %copy-start.4) | copy-done | bytes 56
  1.9 0.1 tile.10
  2.0 0.1 stack_broadcast_in_dim.10
  2.1 0.0 copy-start.2
  2.1 0.1 stack_broadcast_in_dim.24
  2.2 0.6 %copy-done.2 = f32[1,1,8]{2,1,0:T(1,128)S(1)} copy-done((f32[1,1,8]{2,1,0:T(1,128)S(1)}, f32[1,1,8]{2,1,0:T(1,128)}, u32[]{:S(2)}) %copy-start.2) | copy-done | bytes 56
  2.8 0.1 stack_broadcast_in_dim.26
  2.8 0.6 %pad_maximum_fusion.meta = f32[4,8,128]{2,1,0:T(8,128)} fusion(f32[1,8,128]{2,1,0:T(8,128)S(1)} %stack_broadcast_in_dim.26, f32[1,8,128]{2,1,0:T(8,128)S(1)} %stack_broadcast_in_dim.24, f32[1,8,128]{2,1,0:T(8,128)S(1)} %stack_broadcast_in_dim.11, f32[1,8,128]{2,1,0:T(8,128)S(1)} %stack_broadcast_in_dim.10), kind=kLoop, calls=%fused_computation | loop fusion | flops 12288 | bytes 32768 | tf_op jit(solution)/shard_map/stack | solution.py:333
  3.5 39.5 %coupled_window.1 = (bf16[2,128,8,128]{3,2,1,0:T(8,128)(2,1)}, bf16[2,80,8,128]{3,2,1,0:T(8,128)(2,1)}, f32[2,8,128]{2,1,0:T(8,128)}) custom-call(bf16[2,128,8,128]{3,2,1,0:T(8,128)(2,1)} %atm_h.1, bf16[128,8,128]{2,1,0:T(8,128)(2,1)} %acour_h.1, f32[128]{0:T(128)} %adiff_h.1, bf16[2,80,8,128]{3,2,1,0:T(8,128)(2,1)} %ocn_h.1, bf16[80,8,128]{2,1,0:T(8,128)(2,1)} %ocour_h.1, ...), custom_call_target="tpu_custom_call" | custom-call | tf_op jit(solution)/shard_map/coupled_window/pallas_call | solution.py:346
  43.0 0.0 copy-start
  43.0 1.9 %copy.18 = bf16[2,128,8,128]{3,2,1,0:T(8,128)(2,1)} copy(bf16[2,128,8,128]{3,2,1,0:T(8,128)(2,1)} %get-tuple-element.6) | data formatting | bytes 1048576
  44.9 0.0 copy-done
  44.9 0.0 copy-start.1
  44.9 0.7 %copy.19 = bf16[2,80,8,128]{3,2,1,0:T(8,128)(2,1)} copy(bf16[2,80,8,128]{3,2,1,0:T(8,128)(2,1)S(1)} %copy-done) | data formatting | bytes 655360
  45.6 0.0 copy-done.1
  45.6 0.6 %copy.20 = f32[2,8,128]{2,1,0:T(8,128)} copy(f32[2,8,128]{2,1,0:T(8,128)S(1)} %copy-done.1) | data formatting | bytes 16384
  (5 shorter events, 0.0 us)
Async XLA Ops:
  0.6 0.7 %copy-start.3 = (s32[1,1,8,1]{2,3,1,0:T(1,128)S(1)}, s32[1,1,8,1]{2,3,1,0:T(1,128)}, u32[]{:S(2)}) copy-start(s32[1,1,8,1]{2,3,1,0:T(1,128)} %param.20) | copy-start | bytes 100
  1.3 0.7 %copy-start.4 = (s32[1,1,8]{2,1,0:T(1,128)S(1)}, s32[1,1,8]{2,1,0:T(1,128)}, u32[]{:S(2)}) copy-start(s32[1,1,8]{2,1,0:T(1,128)} %param.21) | copy-start | bytes 100
  2.1 0.7 %copy-start.2 = (f32[1,1,8]{2,1,0:T(1,128)S(1)}, f32[1,1,8]{2,1,0:T(1,128)}, u32[]{:S(2)}) copy-start(f32[1,1,8]{2,1,0:T(1,128)} %param.22) | copy-start | bytes 100
  43.0 1.9 %copy-start = (bf16[2,80,8,128]{3,2,1,0:T(8,128)(2,1)S(1)}, bf16[2,80,8,128]{3,2,1,0:T(8,128)(2,1)}, u32[]{:S(2)}) copy-start(bf16[2,80,8,128]{3,2,1,0:T(8,128)(2,1)} %get-tuple-element.7) | copy-start | bytes 983044
  44.9 0.7 %copy-start.1 = (f32[2,8,128]{2,1,0:T(8,128)S(1)}, f32[2,8,128]{2,1,0:T(8,128)}, u32[]{:S(2)}) copy-start(f32[2,8,128]{2,1,0:T(8,128)} %get-tuple-element.8) | copy-start | bytes 24580

commit v2 on v1

--- a/solution.py
+++ b/solution.py
@@ -117,9 +117,10 @@
 
 
 def kernel(
-    atm_h, acour_h, adiff_h, ocn_h, ocour_h, odiff_h, seen_h, bulk_h, mask_h, meta,
+    atm_h, acour_h, adiff_h, ocn_h, ocour_h, odiff_h, seen_h, bulk_h, mask_h,
+    owner_h, slot_h, weight_h,
     atm_o, ocn_o, surf_o,
-    atm_in, acour, adiff, ocn_in, ocour, odiff, seen, bulk, mask,
+    top_in, atm_in, acour, adiff, ocn_in, ocour, odiff, seen, bulk, mask, owner, slots, weights,
     a0m, a0h, a1m, a1h, o0m, o0h, o1m, o1h, acour_e, ocour_e,
     packed, from_left, from_right,
     flux_out, flux_in, reply_out, reply_in, edge_out, edge_left, edge_right,
@@ -140,9 +141,10 @@
         pl.semaphore_signal(barrier, inc=1, device_id=where, device_id_type=MESH)
 
     pairs = [
-        (atm_h, atm_in), (seen_h, seen), (bulk_h, bulk), (acour_h, acour),
-        (ocn_h, ocn_in), (ocour_h, ocour), (mask_h, mask), (adiff_h, adiff),
-        (odiff_h, odiff),
+        (owner_h, owner), (slot_h, slots), (weight_h, weights),
+        (atm_h.at[:, LA - 1], top_in), (seen_h, seen), (bulk_h, bulk),
+        (atm_h, atm_in), (ocn_h, ocn_in), (acour_h, acour),
+        (ocour_h, ocour), (mask_h, mask), (adiff_h, adiff), (odiff_h, odiff),
     ]
     loads = [
         pltpu.make_async_copy(src, dst, in_sem.at[i]) for i, (src, dst) in enumerate(pairs)
@@ -153,26 +155,36 @@
     lane = lane_ids()
     row = lax.broadcasted_iota(jnp.int32, (ROWS, LANES), 0)
 
-    owner_row, owner_lane = meta[0], meta[1]
+    for load in loads[:3]:
+        load.wait()
+    spread = lane < 24
+    owner_row = jnp.zeros((ROWS, LANES), jnp.int32)
+    owner_lane, slot_row = owner_row, owner_row
+    weight = jnp.zeros((ROWS, LANES), F32)
+    for b in range(ROWS):
+        owner_row = jnp.where(row == b, owner[b], owner_row)
+        slot_row = jnp.where(row == b, slots[b], slot_row)
+        weight = jnp.where(row == b, weights[b], weight)
+        owner_lane = jnp.where(lane % 8 == b, owner[b], owner_lane)
+    owner_lane = jnp.where(spread, owner_lane, -1)
     earlier = jnp.sum(
         jnp.where((owner_row == owner_lane) & (row < lane % 8), 1.0, 0.0),
         axis=0,
         keepdims=True,
     )
-    target = 8.0 * owner_lane[0:1] + 2.0 * (lane[0:1] // 8).astype(F32) + earlier
+    target = 8.0 * owner_lane[0:1].astype(F32) + 2.0 * (lane[0:1] // 8).astype(F32) + earlier
     target = jnp.where(lane[0:1] < 24, target, -1.0)
     rows_all = lax.broadcasted_iota(jnp.int32, (8 * SEC, LANES), 0)
     placing = jnp.where(rows_all.astype(F32) == target, 1.0, 0.0)
 
-    for load in loads[:3]:
+    for load in loads[3:6]:
         load.wait()
-    top_t = atm_in[0, LA - 1].astype(F32)
-    top_q = atm_in[1, LA - 1].astype(F32)
+    top_t = top_in[0].astype(F32)
+    top_q = top_in[1].astype(F32)
     heat = bulk[...] * (top_t - seen[0])
     evap = bulk[...] * (0.5 * seen[0] - top_q)
-    weight = meta[3]
     payload = jnp.concatenate(
-        [heat * weight, evap * weight, meta[2] + 1.0, jnp.zeros((LANES - 24, LANES), F32)],
+        [heat * weight, evap * weight, slot_row.astype(F32) + 1.0, jnp.zeros((LANES - 24, LANES), F32)],
         axis=0,
     )
     outgoing = jnp.dot(
@@ -180,20 +192,6 @@
     )
     flux_out[...] = outgoing.reshape(SEC, ROWS, LANES).astype(BF16)
     flux_in[sec] = flux_out[sec]
-
-    widen(atm_in, a0m, LA)
-    a0m[0, LA] = top_t - 0.5 * heat
-    a0m[1, LA] = top_q + 0.5 * evap
-    pad_levels(a0m, LA)
-    for load in loads[3:]:
-        load.wait()
-    widen(ocn_in, o0m, LO)
-    pad_levels(o0m, LO)
-    for f in range(2):
-        pack_edges(lambda l, f=f: a0m[f, l + 1], LA // GROUP, PA + f * LA // GROUP, packed)
-        pack_edges(lambda l, f=f: o0m[f, l + 1], LO // GROUP, PO + f * LO // GROUP, packed)
-    pack_edges(lambda l: acour[l].astype(F32), LA // GROUP, PAC, packed)
-    pack_edges(lambda l: ocour[l].astype(F32), LO // GROUP, POC, packed)
 
     pl.semaphore_wait(barrier, SEC + 1)
 
@@ -216,6 +214,21 @@
     fluxes = [to_sec(k, flux_out, flux_in, flux_ss, flux_rs) for k in order]
     for copy in fluxes:
         copy.start()
+    loads[6].wait()
+    widen(atm_in, a0m, LA)
+    a0m[0, LA] = top_t - 0.5 * heat
+    a0m[1, LA] = top_q + 0.5 * evap
+    pad_levels(a0m, LA)
+    for load in loads[7:]:
+        load.wait()
+    widen(ocn_in, o0m, LO)
+    pad_levels(o0m, LO)
+    for f in range(2):
+        pack_edges(lambda l, f=f: a0m[f, l + 1], LA // GROUP, PA + f * LA // GROUP, packed)
+        pack_edges(lambda l, f=f: o0m[f, l + 1], LO // GROUP, PO + f * LO // GROUP, packed)
+    pack_edges(lambda l: acour[l].astype(F32), LA // GROUP, PAC, packed)
+    pack_edges(lambda l: ocour[l].astype(F32), LO // GROUP, POC, packed)
+
     halos = to_sides(packed, from_left, from_right, halo_ss, halo_rs)
     for copy in halos:
         copy.start()
@@ -328,49 +341,59 @@
     surface_seen, bulk_coeff, flux_owner, flux_slot, flux_weight, ocean_mask,
 ):
     shape = (ROWS, LANES)
-    owner = flux_owner[0, 0, :, 0].astype(F32)
-    by_lane = jnp.pad(jnp.tile(owner, 3), (0, LANES - 24), constant_values=-1.0)
-    meta = jnp.stack(
-        [
-            jnp.broadcast_to(owner[:, None], shape),
-            jnp.broadcast_to(by_lane[None, :], shape),
-            jnp.broadcast_to(flux_slot[0, 0].astype(F32)[:, None], shape),
-            jnp.broadcast_to(flux_weight[0, 0][:, None], shape),
-        ]
-    )
     hbm = pl.BlockSpec(memory_space=pl.ANY)
     vmem = pl.BlockSpec(memory_space=pltpu.VMEM)
     V = pltpu.VMEM
     D = pltpu.SemaphoreType.DMA
     strip_a, strip_o = V((2, LA + 2) + shape, F32), V((2, LO + 2) + shape, F32)
-    return pl.pallas_call(
+    held = (V((2, LA) + shape, BF16), V((2, LO) + shape, BF16), V((2,) + shape, F32))
+    results = pl.pallas_call(
         kernel,
-        out_shape=(
-            jax.ShapeDtypeStruct((2, LA) + shape, BF16),
-            jax.ShapeDtypeStruct((2, LO) + shape, BF16),
-            jax.ShapeDtypeStruct((2,) + shape, F32),
-        ),
-        in_specs=[hbm] * 9 + [vmem],
+        out_shape=held,
+        in_specs=[hbm] * 12,
         out_specs=(vmem, vmem, vmem),
         scratch_shapes=[
+            V((2,) + shape, BF16),
             V((2, LA) + shape, BF16), V((LA,) + shape, BF16), pltpu.SMEM((LA,), F32),
             V((2, LO) + shape, BF16), V((LO,) + shape, BF16), pltpu.SMEM((LO,), F32),
             V((2,) + shape, F32), V(shape, F32), V(shape, jnp.int32),
+            pltpu.SMEM((ROWS,), jnp.int32), pltpu.SMEM((ROWS,), jnp.int32),
+            pltpu.SMEM((ROWS,), F32),
             strip_a, strip_a, strip_a, strip_a, strip_o, strip_o, strip_o, strip_o,
             V((LA,) + shape, F32), V((LO,) + shape, F32),
             V((PACKED,) + shape, BF16), V((PACKED,) + shape, BF16), V((PACKED,) + shape, BF16),
             V((SEC,) + shape, BF16), V((SEC,) + shape, BF16),
             V((SEC,) + shape, BF16), V((SEC,) + shape, BF16),
             V((2,) + shape, BF16), V((2,) + shape, BF16), V((2,) + shape, BF16),
-            D((9,)), D((SEC,)), D((SEC,)), D((SEC,)), D((SEC,)),
+            D((13,)), D((SEC,)), D((SEC,)), D((SEC,)), D((SEC,)),
             D((2,)), D((2,)), D((2,)), D((2,)),
         ],
         compiler_params=pltpu.CompilerParams(collective_id=0, has_side_effects=True),
         name="coupled_window",
     )(
         atm_tracers, atm_courant, atm_diffusion, ocean_tracers, ocean_courant,
-        ocean_diffusion, surface_seen, bulk_coeff, ocean_mask, meta,
-    )
+        ocean_diffusion, surface_seen, bulk_coeff, ocean_mask,
+        flux_owner.reshape(ROWS), flux_slot.reshape(ROWS), flux_weight.reshape(ROWS),
+    )
+    return pl.pallas_call(
+        put_out,
+        out_shape=tuple(jax.ShapeDtypeStruct(r.shape, r.dtype) for r in results),
+        in_specs=[vmem] * 3,
+        out_specs=(hbm, hbm, hbm),
+        scratch_shapes=[D((3,))],
+        name="put_out",
+    )(*[pltpu.with_memory_space_constraint(r, pltpu.VMEM) for r in results])
+
+
+def put_out(a_ref, o_ref, s_ref, a_out, o_out, s_out, sems):
+    copies = [
+        pltpu.make_async_copy(src, dst, sems.at[i])
+        for i, (src, dst) in enumerate(((a_ref, a_out), (o_ref, o_out), (s_ref, s_out)))
+    ]
+    for copy in copies:
+        copy.start()
+    for copy in copies:
+        copy.wait()
 
 
 def solution(mesh):

time: 46.6 us -> 43.4 us (0.931)
  local copies, waits for them, and re-layouts: 5.44 us -> 0 us
  Pallas kernels: 39.5 us -> 42.6 us
  other arithmetic: 0.61 us -> 0 us
    unnamed x13 -> x0, local copies, waits for them, and re-layouts: 5.13 us -> none
    pallas_call x1 -> x2, Pallas kernels: 39.5 us -> 42.6 us  [the longest x1 41.7 us: body(): pl.pallas_call(kernel, out_shape=held, in_specs=[hbm] * 12, out_specs=(vm...]
    another operation x1 -> x0, other arithmetic: 0.61 us -> none  [body(): jnp.stack([jnp.broadcast_to(owner[:, None], shape), jnp.broadcast_to(by_l...]
where the time goes in v2:
time: 43.4 us; the launch traced here: 43.3 us
  Pallas kernels  42.6 us (98%)
  between operations  0.64 us (1%)
    pallas_call x1, Pallas kernels, body(): pl.pallas_call(kernel, out_shape=held, in_specs=[hbm] * 12, out_specs=(vm...  41.7 us
    pallas_call x1, Pallas kernels, body(): pl.pallas_call(put_out, out_shape=tuple((jax.ShapeDtypeStruct(r.shape, r....  0.93 us

profile of v2, /device:TPU:1, one launch (start us, length us, event | category | flops | bytes accessed | tf_op | source)
XLA Modules:
  0.0 43.3 jit_solution(17234081247203321487)
XLA Ops:
  0.6 41.7 %coupled_window.1 = (bf16[2,128,8,128]{3,2,1,0:T(8,128)(2,1)S(1)}, bf16[2,80,8,128]{3,2,1,0:T(8,128)(2,1)S(1)}, f32[2,8,128]{2,1,0:T(8,128)S(1)}) custom-call(bf16[2,128,8,128]{3,2,1,0:T(8,128)(2,1)} %atm_h.1, bf16[128,8,128]{2,1,0:T(8,128)(2,1)} %acour_h.1, f32[128]{0:T(128)} %adiff_h.1, bf16[2,80,8,128]{3,2,1,0:T(8,128)(2,1)} %ocn_h.1, ...), custom_call_target="tpu_custom_call" | custom-call | tf_op jit(solution)/shard_map/coupled_window/pallas_call | solution.py:350
  42.3 0.9 %put_out.1 = (bf16[2,128,8,128]{3,2,1,0:T(8,128)(2,1)}, bf16[2,80,8,128]{3,2,1,0:T(8,128)(2,1)}, f32[2,8,128]{2,1,0:T(8,128)}) custom-call(bf16[2,128,8,128]{3,2,1,0:T(8,128)(2,1)S(1)} %get-tuple-element.6.a_ref, bf16[2,80,8,128]{3,2,1,0:T(8,128)(2,1)S(1)} %get-tuple-element.7.o_ref, f32[2,8,128]{2,1,0:T(8,128)S(1)} %get-tuple-element.8.s_ref), custom_call_target="tpu_custom_call" | custom-call | tf_op jit(solution)/shard_map/put_out/pallas_call | solution.py:378

commit v3 on v2

--- a/solution.py
+++ b/solution.py
@@ -14,7 +14,7 @@
 LA = 128
 LO = 80
 GROUP = 16
-CHUNK = 8
+CHUNK = 16
 F32 = jnp.float32
 BF16 = jnp.bfloat16
 MESH = pl.DeviceIdType.MESH
@@ -193,27 +193,6 @@
     flux_out[...] = outgoing.reshape(SEC, ROWS, LANES).astype(BF16)
     flux_in[sec] = flux_out[sec]
 
-    pl.semaphore_wait(barrier, SEC + 1)
-
-    def to_sec(k, src, dst, ss, rs):
-        peer = lax.rem(sec + k, SEC)
-        return pltpu.make_async_remote_copy(
-            src_ref=src.at[peer], dst_ref=dst.at[sec], send_sem=ss.at[k], recv_sem=rs.at[k],
-            device_id=(peer, tile), device_id_type=MESH,
-        )
-
-    def to_sides(src, at_left, at_right, ss, rs):
-        return [
-            pltpu.make_async_remote_copy(
-                src_ref=src, dst_ref=dst, send_sem=ss.at[i], recv_sem=rs.at[i],
-                device_id=where, device_id_type=MESH,
-            )
-            for i, (dst, where) in enumerate(((at_left, to_right), (at_right, to_left)))
-        ]
-
-    fluxes = [to_sec(k, flux_out, flux_in, flux_ss, flux_rs) for k in order]
-    for copy in fluxes:
-        copy.start()
     loads[6].wait()
     widen(atm_in, a0m, LA)
     a0m[0, LA] = top_t - 0.5 * heat
@@ -229,6 +208,27 @@
     pack_edges(lambda l: acour[l].astype(F32), LA // GROUP, PAC, packed)
     pack_edges(lambda l: ocour[l].astype(F32), LO // GROUP, POC, packed)
 
+    pl.semaphore_wait(barrier, SEC + 1)
+
+    def to_sec(k, src, dst, ss, rs, used):
+        peer = lax.rem(sec + k, SEC)
+        return pltpu.make_async_remote_copy(
+            src_ref=src.at[peer, 0:used], dst_ref=dst.at[sec, 0:used], send_sem=ss.at[k], recv_sem=rs.at[k],
+            device_id=(peer, tile), device_id_type=MESH,
+        )
+
+    def to_sides(src, at_left, at_right, ss, rs):
+        return [
+            pltpu.make_async_remote_copy(
+                src_ref=src, dst_ref=dst, send_sem=ss.at[i], recv_sem=rs.at[i],
+                device_id=where, device_id_type=MESH,
+            )
+            for i, (dst, where) in enumerate(((at_left, to_right), (at_right, to_left)))
+        ]
+
+    fluxes = [to_sec(k, flux_out, flux_in, flux_ss, flux_rs, 6) for k in order]
+    for copy in fluxes:
+        copy.start()
     halos = to_sides(packed, from_left, from_right, halo_ss, halo_rs)
     for copy in halos:
         copy.start()
@@ -256,15 +256,11 @@
     unpack_edges(put_oc, LO // GROUP, POC, from_left, from_right)
     pad_levels(o0h, LO)
     step_levels(o0m, o0h, o1m, o1h, ocour, ocour_e, odiff, LO)
-    for f in range(2):
-        unpack_edges(put_a(f), LA // GROUP, PA + f * LA // GROUP, from_left, from_right)
-    unpack_edges(put_ac, LA // GROUP, PAC, from_left, from_right)
-    pad_levels(a0h, LA)
-    step_levels(a0m, a0h, a1m, a1h, acour, acour_e, adiff, LA)
 
     for copy in fluxes:
         copy.wait()
     arrived = flux_in[...].astype(F32).reshape(8 * SEC, LANES)
+    arrived = jnp.where(rows_all % 8 < 6, arrived, 0.0)
     lane_all = lax.broadcasted_iota(jnp.int32, (8 * SEC, LANES), 1)
     kind = rows_all % 8
     up2 = pltpu.roll(arrived, 8 * SEC - 2, 0)
@@ -289,6 +285,10 @@
     edges = to_sides(edge_out, edge_left, edge_right, edge_ss, edge_rs)
     for copy in edges:
         copy.start()
+    for f in range(2):
+        unpack_edges(put_a(f), LA // GROUP, PA + f * LA // GROUP, from_left, from_right)
+    unpack_edges(put_ac, LA // GROUP, PAC, from_left, from_right)
+    pad_levels(a0h, LA)
     for copy in edges:
         copy.wait()
     for f in range(2):
@@ -316,18 +316,20 @@
     rows_top = jnp.concatenate(tops + [jnp.zeros((LANES - 16, LANES), F32)], axis=0)
     answers = jnp.dot(collect.astype(BF16), rows_top.astype(BF16), preferred_element_type=F32)
     reply_out[...] = answers.reshape(SEC, ROWS, LANES).astype(BF16)
-    replies = [to_sec(k, reply_out, reply_in, reply_ss, reply_rs) for k in order]
+    replies = [to_sec(k, reply_out, reply_in, reply_ss, reply_rs, 4) for k in order]
     for copy in replies:
         copy.start()
     reply_in[sec] = reply_out[sec]
 
     step_levels(o1m, o1h, None, None, ocour, ocour_e, odiff, LO, ocn_o)
+    step_levels(a0m, a0h, a1m, a1h, acour, acour_e, adiff, LA)
     step_levels(a1m, a1h, a0m, a0h, acour, acour_e, adiff, LA)
     step_levels(a0m, a0h, None, None, acour, acour_e, adiff, LA, atm_o)
 
     for copy in replies:
         copy.wait()
     back = reply_in[...].astype(F32).reshape(8 * SEC, LANES)
+    back = jnp.where(kind < 4, back, 0.0)
     surface = lax.dot_general(
         placing.astype(BF16), back.astype(BF16), (((0,), (0,)), ((), ())),
         preferred_element_type=F32,

time: 43.4 us -> 35.3 us (0.81)
  Pallas kernels: 42.6 us -> 34.5 us
    pallas_call x1, Pallas kernels: 41.7 us -> 33.6 us  [body(): pl.pallas_call(kernel, out_shape=held, in_specs=[hbm] * 12, out_specs=(vm...]
where the time goes in v3:
time: 35.3 us; the launch traced here: 35.1 us
  Pallas kernels  34.5 us (98%)
  between operations  0.64 us (2%)
    pallas_call x1, Pallas kernels, body(): pl.pallas_call(kernel, out_shape=held, in_specs=[hbm] * 12, out_specs=(vm...  33.6 us
    pallas_call x1, Pallas kernels, body(): pl.pallas_call(put_out, out_shape=tuple((jax.ShapeDtypeStruct(r.shape, r....  0.93 us

profile of v3, /device:TPU:1, one launch (start us, length us, event | category | flops | bytes accessed | tf_op | source)
XLA Modules:
  0.0 35.1 jit_solution(1214039352331456464)
XLA Ops:
  0.6 33.6 %coupled_window.1 = (bf16[2,128,8,128]{3,2,1,0:T(8,128)(2,1)S(1)}, bf16[2,80,8,128]{3,2,1,0:T(8,128)(2,1)S(1)}, f32[2,8,128]{2,1,0:T(8,128)S(1)}) custom-call(bf16[2,128,8,128]{3,2,1,0:T(8,128)(2,1)} %atm_h.1, bf16[128,8,128]{2,1,0:T(8,128)(2,1)} %acour_h.1, f32[128]{0:T(128)} %adiff_h.1, bf16[2,80,8,128]{3,2,1,0:T(8,128)(2,1)} %ocn_h.1, ...), custom_call_target="tpu_custom_call" | custom-call | tf_op jit(solution)/shard_map/coupled_window/pallas_call | solution.py:352
  34.2 0.9 %put_out.1 = (bf16[2,128,8,128]{3,2,1,0:T(8,128)(2,1)}, bf16[2,80,8,128]{3,2,1,0:T(8,128)(2,1)}, f32[2,8,128]{2,1,0:T(8,128)}) custom-call(bf16[2,128,8,128]{3,2,1,0:T(8,128)(2,1)S(1)} %get-tuple-element.6.a_ref, bf16[2,80,8,128]{3,2,1,0:T(8,128)(2,1)S(1)} %get-tuple-element.7.o_ref, f32[2,8,128]{2,1,0:T(8,128)S(1)} %get-tuple-element.8.s_ref), custom_call_target="tpu_custom_call" | custom-call | tf_op jit(solution)/shard_map/put_out/pallas_call | solution.py:380

commit v4 on v3

--- a/solution.py
+++ b/solution.py
@@ -19,8 +19,10 @@
 BF16 = jnp.bfloat16
 MESH = pl.DeviceIdType.MESH
 
-PA, PAC, PO, POC = 0, 2 * LA // GROUP, 3 * LA // GROUP, (3 * LA + 2 * LO) // GROUP
-PACKED = (3 * LA + 3 * LO) // GROUP
+PO, POC, PACKED = 0, 2 * LO // GROUP, 3 * LO // GROUP
+WIN = 16
+PER = LANES // WIN
+GA = LA // PER
 
 
 def lane_ids():
@@ -116,15 +118,106 @@
             store(i * GROUP + j, pltpu.roll(both, (LANES - 8 * j - 4) % LANES, 1))
 
 
+def strip_steps(src, dst, c_ref, k_ref, levels):
+    @pl.loop(0, levels // CHUNK)
+    def _(i):
+        for g in range(CHUNK):
+            l = i * CHUNK + g
+            c = c_ref[l].astype(F32)
+            k = k_ref[l]
+            for f in range(2):
+                m = src[f, l + 1]
+                right, left = pltpu.roll(m, LANES - 1, 1), pltpu.roll(m, 1, 1)
+                dst[f, l + 1] = cell_step(m, src[f, l], src[f, l + 2], right, left, c, k)
+
+    pad_levels(dst, levels)
+
+
+def pack_windows(read, base, wide):
+    @pl.loop(0, GA // 2)
+    def _(i):
+        part = lane_ids() // WIN
+        for h in range(2):
+            acc = jnp.zeros((ROWS, LANES), F32)
+            for j in range(PER):
+                shift = (WIN * j + WIN // 2) % LANES
+                rolled = pltpu.roll(read((2 * i + h) * PER + j), shift, 1)
+                acc = jnp.where(part == j, rolled, acc)
+            wide[base + 2 * i + h] = acc.astype(BF16)
+
+
+def pad_seams(ref):
+    for x in range(2):
+        for f in range(2):
+            ref[x, f, 0] = pltpu.roll(ref[x, f, 1], LANES - WIN, 1)
+            ref[x, f, GA + 1] = pltpu.roll(ref[x, f, GA], WIN, 1)
+
+
+def open_seams(wide, wide_left, wide_right, seams, speeds, k_ref, k_tiles):
+    @pl.loop(0, GA)
+    def _(i):
+        lane = lane_ids()
+        first = lane % WIN < WIN // 2
+        for n in range(3):
+            own = wide[n * GA + i].astype(F32)
+            at_left = jnp.where(first, wide_left[n * GA + i].astype(F32), own)
+            at_right = jnp.where(first, own, wide_right[n * GA + i].astype(F32))
+            if n < 2:
+                seams[0, n, i + 1] = at_left
+                seams[1, n, i + 1] = at_right
+            else:
+                speeds[0, i] = at_left
+                speeds[1, i] = at_right
+        k = jnp.zeros((ROWS, LANES), F32)
+        for j in range(PER):
+            k = jnp.where(lane // WIN == j, k_ref[i * PER + j], k)
+        k_tiles[i] = k
+
+    pad_seams(seams)
+
+
+def seam_steps(src, dst, speeds, k_tiles):
+    @pl.loop(0, GA // 2)
+    def _(h):
+        lane = lane_ids()
+        for i in (2 * h, 2 * h + 1):
+            k = k_tiles[i]
+            for x in range(2):
+                c = speeds[x, i]
+                for f in range(2):
+                    q = src[x, f, i + 1]
+                    above = jnp.where(lane >= LANES - WIN, src[x, f, i], q)
+                    below = jnp.where(lane < WIN, src[x, f, i + 2], q)
+                    dst[x, f, i + 1] = cell_step(
+                        q, pltpu.roll(above, WIN, 1), pltpu.roll(below, LANES - WIN, 1),
+                        pltpu.roll(q, LANES - 1, 1), pltpu.roll(q, 1, 1), c, k,
+                    )
+
+    pad_seams(dst)
+
+
+def close_seams(strip, seams, out):
+    @pl.loop(0, GA)
+    def _(i):
+        lane = lane_ids()
+        edge = (lane < ATM_STEPS) | (lane >= LANES - ATM_STEPS)
+        for f in range(2):
+            own = jnp.where(lane % WIN < WIN // 2, seams[1, f, i + 1], seams[0, f, i + 1])
+            for j in range(PER):
+                l = i * PER + j
+                rolled = pltpu.roll(own, (LANES - WIN * j - WIN // 2) % LANES, 1)
+                out[f, l] = jnp.where(edge, rolled, strip[f, l + 1]).astype(BF16)
+
+
 def kernel(
     atm_h, acour_h, adiff_h, ocn_h, ocour_h, odiff_h, seen_h, bulk_h, mask_h,
     owner_h, slot_h, weight_h,
     atm_o, ocn_o, surf_o,
     top_in, atm_in, acour, adiff, ocn_in, ocour, odiff, seen, bulk, mask, owner, slots, weights,
-    a0m, a0h, a1m, a1h, o0m, o0h, o1m, o1h, acour_e, ocour_e,
-    packed, from_left, from_right,
+    a0m, a1m, o0m, o0h, o1m, o1h, ocour_e, seam0, seam1, speeds, k_tiles,
+    packed, from_left, from_right, wide, wide_left, wide_right,
     flux_out, flux_in, reply_out, reply_in, edge_out, edge_left, edge_right,
-    in_sem, flux_ss, flux_rs, reply_ss, reply_rs, halo_ss, halo_rs, edge_ss, edge_rs,
+    in_sem, flux_ss, flux_rs, reply_ss, reply_rs, halo_ss, halo_rs, wide_ss, wide_rs, edge_ss, edge_rs,
 ):
     sec = lax.axis_index("sec")
     tile = lax.axis_index("tile")
@@ -203,9 +296,9 @@
     widen(ocn_in, o0m, LO)
     pad_levels(o0m, LO)
     for f in range(2):
-        pack_edges(lambda l, f=f: a0m[f, l + 1], LA // GROUP, PA + f * LA // GROUP, packed)
+        pack_windows(lambda l, f=f: a0m[f, l + 1], f * GA, wide)
         pack_edges(lambda l, f=f: o0m[f, l + 1], LO // GROUP, PO + f * LO // GROUP, packed)
-    pack_edges(lambda l: acour[l].astype(F32), LA // GROUP, PAC, packed)
+    pack_windows(lambda l: acour[l].astype(F32), 2 * GA, wide)
     pack_edges(lambda l: ocour[l].astype(F32), LO // GROUP, POC, packed)
 
     pl.semaphore_wait(barrier, SEC + 1)
@@ -232,22 +325,20 @@
     halos = to_sides(packed, from_left, from_right, halo_ss, halo_rs)
     for copy in halos:
         copy.start()
+    sides = to_sides(wide, wide_left, wide_right, wide_ss, wide_rs)
+    for copy in sides:
+        copy.start()
+    strip_steps(a0m, a1m, acour, adiff, LA)
+    strip_steps(a1m, a0m, acour, adiff, LA)
+    strip_steps(a0m, a1m, acour, adiff, LA)
     for copy in halos:
         copy.wait()
-
-    def put_a(f):
-        def store(l, value):
-            a0h[f, l + 1] = value
-        return store
 
     def put_o(f):
         def store(l, value):
             o0h[f, l + 1] = value
         return store
 
-    def put_ac(l, value):
-        acour_e[l] = value
-
     def put_oc(l, value):
         ocour_e[l] = value
 
@@ -255,7 +346,6 @@
         unpack_edges(put_o(f), LO // GROUP, PO + f * LO // GROUP, from_left, from_right)
     unpack_edges(put_oc, LO // GROUP, POC, from_left, from_right)
     pad_levels(o0h, LO)
-    step_levels(o0m, o0h, o1m, o1h, ocour, ocour_e, odiff, LO)
 
     for copy in fluxes:
         copy.wait()
@@ -285,10 +375,7 @@
     edges = to_sides(edge_out, edge_left, edge_right, edge_ss, edge_rs)
     for copy in edges:
         copy.start()
-    for f in range(2):
-        unpack_edges(put_a(f), LA // GROUP, PA + f * LA // GROUP, from_left, from_right)
-    unpack_edges(put_ac, LA // GROUP, PAC, from_left, from_right)
-    pad_levels(a0h, LA)
+    step_levels(o0m, o0h, o1m, o1h, ocour, ocour_e, odiff, LO)
     for copy in edges:
         copy.wait()
     for f in range(2):
@@ -322,10 +409,13 @@
     reply_in[sec] = reply_out[sec]
 
     step_levels(o1m, o1h, None, None, ocour, ocour_e, odiff, LO, ocn_o)
-    step_levels(a0m, a0h, a1m, a1h, acour, acour_e, adiff, LA)
-    step_levels(a1m, a1h, a0m, a0h, acour, acour_e, adiff, LA)
-    step_levels(a0m, a0h, None, None, acour, acour_e, adiff, LA, atm_o)
-
+    for copy in sides:
+        copy.wait()
+    open_seams(wide, wide_left, wide_right, seam0, speeds, adiff, k_tiles)
+    seam_steps(seam0, seam1, speeds, k_tiles)
+    seam_steps(seam1, seam0, speeds, k_tiles)
+    seam_steps(seam0, seam1, speeds, k_tiles)
+    close_seams(a1m, seam1, atm_o)
     for copy in replies:
         copy.wait()
     back = reply_in[...].astype(F32).reshape(8 * SEC, LANES)
@@ -347,6 +437,7 @@
     vmem = pl.BlockSpec(memory_space=pltpu.VMEM)
     V = pltpu.VMEM
     D = pltpu.SemaphoreType.DMA
+    seam = V((2, 2, GA + 2) + shape, F32)
     strip_a, strip_o = V((2, LA + 2) + shape, F32), V((2, LO + 2) + shape, F32)
     held = (V((2, LA) + shape, BF16), V((2, LO) + shape, BF16), V((2,) + shape, F32))
     results = pl.pallas_call(
@@ -361,14 +452,15 @@
             V((2,) + shape, F32), V(shape, F32), V(shape, jnp.int32),
             pltpu.SMEM((ROWS,), jnp.int32), pltpu.SMEM((ROWS,), jnp.int32),
             pltpu.SMEM((ROWS,), F32),
-            strip_a, strip_a, strip_a, strip_a, strip_o, strip_o, strip_o, strip_o,
-            V((LA,) + shape, F32), V((LO,) + shape, F32),
+            strip_a, strip_a, strip_o, strip_o, strip_o, strip_o, V((LO,) + shape, F32),
+            seam, seam, V((2, GA) + shape, F32), V((GA,) + shape, F32),
             V((PACKED,) + shape, BF16), V((PACKED,) + shape, BF16), V((PACKED,) + shape, BF16),
+            V((3 * GA,) + shape, BF16), V((3 * GA,) + shape, BF16), V((3 * GA,) + shape, BF16),
             V((SEC,) + shape, BF16), V((SEC,) + shape, BF16),
             V((SEC,) + shape, BF16), V((SEC,) + shape, BF16),
             V((2,) + shape, BF16), V((2,) + shape, BF16), V((2,) + shape, BF16),
             D((13,)), D((SEC,)), D((SEC,)), D((SEC,)), D((SEC,)),
-            D((2,)), D((2,)), D((2,)), D((2,)),
+            D((2,)), D((2,)), D((2,)), D((2,)), D((2,)), D((2,)),
         ],
         compiler_params=pltpu.CompilerParams(collective_id=0, has_side_effects=True),
         name="coupled_window",

time: 35.3 us -> 34.1 us (0.966); the launches traced: 35.1 us -> 33.6 us
  Pallas kernels: 34.5 us -> 32.9 us
    pallas_call x1, Pallas kernels: 33.6 us -> 32 us  [body(): pl.pallas_call(kernel, out_shape=held, in_specs=[hbm] * 12, out_specs=(vm...]
where the time goes in v4:
time: 34.1 us; the launch traced here: 33.6 us
  Pallas kernels  32.9 us (96%)
  between operations  0.64 us (2%)
    pallas_call x1, Pallas kernels, body(): pl.pallas_call(kernel, out_shape=held, in_specs=[hbm] * 12, out_specs=(vm...  32 us
    pallas_call x1, Pallas kernels, body(): pl.pallas_call(put_out, out_shape=tuple((jax.ShapeDtypeStruct(r.shape, r....  0.93 us

profile of v4, /device:TPU:1, one launch (start us, length us, event | category | flops | bytes accessed | tf_op | source)
XLA Modules:
  0.0 33.6 jit_solution(8858388546605619455)
XLA Ops:
  0.6 32.0 %coupled_window.1 = (bf16[2,128,8,128]{3,2,1,0:T(8,128)(2,1)S(1)}, bf16[2,80,8,128]{3,2,1,0:T(8,128)(2,1)S(1)}, f32[2,8,128]{2,1,0:T(8,128)S(1)}) custom-call(bf16[2,128,8,128]{3,2,1,0:T(8,128)(2,1)} %atm_h.1, bf16[128,8,128]{2,1,0:T(8,128)(2,1)} %acour_h.1, f32[128]{0:T(128)} %adiff_h.1, bf16[2,80,8,128]{3,2,1,0:T(8,128)(2,1)} %ocn_h.1, ...), custom_call_target="tpu_custom_call" | custom-call | tf_op jit(solution)/shard_map/coupled_window/pallas_call | solution.py:443
  32.6 0.9 %put_out.1 = (bf16[2,128,8,128]{3,2,1,0:T(8,128)(2,1)}, bf16[2,80,8,128]{3,2,1,0:T(8,128)(2,1)}, f32[2,8,128]{2,1,0:T(8,128)}) custom-call(bf16[2,128,8,128]{3,2,1,0:T(8,128)(2,1)S(1)} %get-tuple-element.6.a_ref, bf16[2,80,8,128]{3,2,1,0:T(8,128)(2,1)S(1)} %get-tuple-element.7.o_ref, f32[2,8,128]{2,1,0:T(8,128)S(1)} %get-tuple-element.8.s_ref), custom_call_target="tpu_custom_call" | custom-call | tf_op jit(solution)/shard_map/put_out/pallas_call | solution.py:472
